TPU v7x, 32 devices: a whole 2x2x4 slice. The times are simulated.
32 devices in a mesh: rep: 4 (over x, core), shard: 8 (over z, y).
Axes of the slice: x: 2, y: 2, z: 4, core: 2. Of those that a mesh axis runs over, the one named last changes fastest.
Arguments:
- inputs: bfloat16 [64, 750, 512], P(('rep', 'shard')), may hold values from -48 to 48
- cotangent: float32 [64, 750, 512], P(('rep', 'shard')), may hold values from -6 to 6
- row_weights: bfloat16 [512, 8192], P('shard'), may hold values from -1.41421356 to 1.41421356
- down_weights: bfloat16 [2, 2048, 512], P(None, 'shard'), may hold values from -0.125 to 0.125
- hidden_bias: bfloat16 [2, 2048], P(None, 'shard'), may hold values from -0.5 to 0.5
- vectors: bfloat16 [53, 512], P(None, 'shard'), may hold values from -1 to 2
- row_first: float32 [512, 8192], P('shard'), may hold values from -64 to 64
- down_first: float32 [2, 2048, 512], P(None, 'shard'), may hold values from -64 to 64
- hidden_first: float32 [2, 2048], P(None, 'shard'), may hold values from -64 to 64
- vector_first: float32 [53, 512], P(None, 'shard'), may hold values from -64 to 64
- row_second: float32 [512, 8192], P('shard'), may hold values from 24 to 240
- down_second: float32 [2, 2048, 512], P(None, 'shard'), may hold values from 24 to 240
- hidden_second: float32 [2, 2048], P(None, 'shard'), may hold values from 24 to 240
- vector_second: float32 [53, 512], P(None, 'shard'), may hold values from 24 to 240
- step_number: int32 [1], replicated, may hold values from 1 to 20
Outputs:
- outputs: float32 [64, 750, 512], P(('rep', 'shard'))
- input_grad: float32 [64, 750, 512], P(('rep', 'shard'))
- row_grad: float32 [512, 8192], P('shard')
- down_grad: float32 [2, 2048, 512], P(None, 'shard')
- hidden_grad: float32 [2, 2048], P(None, 'shard')
- vector_grad: float32 [53, 512], P(None, 'shard')
- row_first_new: float32 [512, 8192], P('shard')
- down_first_new: float32 [2, 2048, 512], P(None, 'shard')
- hidden_first_new: float32 [2, 2048], P(None, 'shard')
- vector_first_new: float32 [53, 512], P(None, 'shard')
- row_second_new: float32 [512, 8192], P('shard')
- down_second_new: float32 [2, 2048, 512], P(None, 'shard')
- hidden_second_new: float32 [2, 2048], P(None, 'shard')
- vector_second_new: float32 [53, 512], P(None, 'shard')
- row_update: float32 [512, 8192], P('shard')
- down_update: float32 [2, 2048, 512], P(None, 'shard')
- hidden_update: float32 [2, 2048], P(None, 'shard')
- vector_update: float32 [53, 512], P(None, 'shard')
All inputs are finite; a program needn't handle non-finite values.
Results may differ from a plain program's by a relative error of at most 0.018.
Values may be sent and summed in bfloat16 or wider, within the bound.
No kernel may reach another device: no remote copies, remote signals or barrier semaphores. Data moves between devices by JAX's collectives and lax.ppermute only.
A program may use at most 384 MiB of HBM per device.

v0:
```python
import math

import jax
import jax.numpy as jnp
from jax import lax
from jax.experimental import pallas as pl
from jax.experimental.pallas import tpu as pltpu
from jax.sharding import PartitionSpec as P

D = 512
HEADS = 8
HEAD = 64
FF = 2048
KERNEL = 31
CLIP_LEN = 750
ROWS = 768
HALF = D // 2
PAIR = 2 * HEAD
PAIRS = HEADS // 2


norm_eps = 1e-05
beta_first = 0.9
beta_second = 0.99
learn_rate = 0.01
weight_decay = 0.1
adam_eps = 1e-08
front_gain = 0
attend_gain = 3
attend_shift = 4
query_bias = 5
value_bias = 6
attend_out = 7
content_bias = 8
position_bias = 9
conv_gain = 10
conv_shift = 11
glu_value = 12
glu_gate = 13
conv_out = 14
batch_gain = 15
batch_shift = 16
back_gain = 17
final_gain = 20
final_shift = 21
kernel_start = 22


def product(left, right):
    return jnp.dot(left, right, preferred_element_type=jnp.float32)


def left_factor(left, right):
    return lax.dot_general(
        left, right, (((0,), (0,)), ((), ())), preferred_element_type=jnp.float32
    )


def product_right(left, right):
    return lax.dot_general(
        left, right, (((1,), (1,)), ((), ())), preferred_element_type=jnp.float32
    )


def swish_act(values):
    return values * jax.nn.sigmoid(values)


def swish_slope(values):
    logistic = jax.nn.sigmoid(values)
    return logistic * (1.0 + values * (1.0 - logistic))


def norm_forward(residual, gain_vec, shift_vec):
    average = jnp.mean(residual, axis=-1, keepdims=True)
    centered = residual - average
    spread = jnp.mean(centered * centered, axis=-1, keepdims=True)
    inverse = lax.rsqrt(spread + norm_eps)
    unit_field = centered * inverse
    return (unit_field * gain_vec + shift_vec, unit_field, inverse)


def norm_backward(grad_out, unit_field, inverse, gain_vec):
    grad_unit = grad_out * gain_vec
    grad_field = inverse * (
        grad_unit
        - jnp.mean(grad_unit, axis=-1, keepdims=True)
        - unit_field * jnp.mean(grad_unit * unit_field, axis=-1, keepdims=True)
    )
    return (grad_field, jnp.sum(grad_out * unit_field, axis=0), jnp.sum(grad_out, axis=0))


def angle_tables():
    frequency = jnp.exp(jnp.arange(0, D, 2).astype(jnp.float32) * (-math.log(10000.0) / D))
    coarse = (32 * jnp.arange(ROWS // 32)).astype(jnp.float32)[:, None] * frequency
    fine = jnp.arange(32).astype(jnp.float32)[:, None] * frequency
    sin_c, cos_c = jnp.sin(coarse)[:, None], jnp.cos(coarse)[:, None]
    sin_f, cos_f = jnp.sin(fine)[None], jnp.cos(fine)[None]
    sine = (sin_c * cos_f + cos_c * sin_f).reshape(ROWS, HALF)
    cosine = (cos_c * cos_f - sin_c * sin_f).reshape(ROWS, HALF)
    stacked = (jnp.concatenate([cosine, sine], axis=1) * HEAD**-0.5).astype(jnp.bfloat16)
    return sine.T, cosine.T, stacked, stacked.T


def dot_nn(left, right):
    return lax.dot_general(
        left, right, (((1,), (0,)), ((), ())), preferred_element_type=jnp.float32
    )


def head_mask(values, head):
    lane = lax.broadcasted_iota(jnp.int32, values.shape, 1)
    inside = lane < HEAD if head == 0 else lane >= HEAD
    return jnp.where(inside, values, jnp.zeros_like(values))


def head_scores(query_content, query_position, keys_scaled, place, sine, cosine, stacked):
    lifted = product_right(place, query_position)
    lift_s, lift_c = lifted[:HALF], lifted[HALF:]
    turned = jnp.concatenate(
        [lift_s * sine + lift_c * cosine, lift_c * sine - lift_s * cosine], axis=0
    ).astype(jnp.bfloat16)
    return product_right(keys_scaled, query_content) + dot_nn(stacked, turned)


def key_valid():
    return lax.broadcasted_iota(jnp.int32, (ROWS, ROWS), 0) < CLIP_LEN


def attend_kernel(
    content_ref, position_ref, key_ref, value_ref, place_ref, sine_ref, cosine_ref, stacked_ref,
    context_ref, total_ref,
):
    query_content, query_position = content_ref[0], position_ref[0]
    keys = key_ref[0] * jnp.bfloat16(HEAD**-0.5)
    values = value_ref[0]
    place = place_ref[...]
    parts = []
    for head in range(2):
        scores = head_scores(
            query_content,
            query_position,
            head_mask(keys, head),
            head_mask(place, head),
            sine_ref[...],
            cosine_ref[...],
            stacked_ref[...],
        )
        scores = jnp.where(key_valid(), scores, -1e30)
        largest = jnp.max(scores, axis=0, keepdims=True)
        weights = jnp.exp(scores - largest)
        total = jnp.sum(weights, axis=0, keepdims=True)
        mixed = left_factor(values, weights.astype(jnp.bfloat16)) * (1.0 / total)
        parts.append(mixed[:HEAD] if head == 0 else mixed[HEAD:])
        total_ref[0, 0, head : head + 1, :] = largest + jnp.log(total)
    context_ref[0] = jnp.concatenate(parts, axis=0).T.astype(jnp.bfloat16)


def attend_back_kernel(
    content_ref, position_ref, key_ref, value_ref, grad_ref, total_ref, place_ref, sine_ref,
    cosine_ref, stacked_ref, stacked_t_ref,
    grad_query_ref, grad_key_ref, grad_value_ref, sums_ref, grad_place_ref,
):
    query_content, query_position = content_ref[0], position_ref[0]
    keys = key_ref[0] * jnp.bfloat16(HEAD**-0.5)
    values = value_ref[0]
    grad_context = grad_ref[0]
    place = place_ref[...]
    sine, cosine = sine_ref[...], cosine_ref[...]
    content_parts, position_parts = [], []
    grad_keys = grad_values = grad_place = None
    for head in range(2):
        keys_head, place_head = head_mask(keys, head), head_mask(place, head)
        scores = head_scores(
            query_content, query_position, keys_head, place_head, sine, cosine, stacked_ref[...]
        )
        weights = jnp.where(
            key_valid(), jnp.exp(scores - total_ref[0, 0, head : head + 1, :]), 0.0
        )
        grad_head = head_mask(grad_context, head)
        grad_weights = product_right(values, grad_head)
        value_part = dot_nn(weights.astype(jnp.bfloat16), grad_head)
        leaning = weights * grad_weights
        delta = jnp.sum(leaning, axis=0, keepdims=True)
        grad_scores = (leaning - weights * delta).astype(jnp.bfloat16)
        content_head = head_mask(query_content, head) * jnp.bfloat16(HEAD**-0.5)
        key_part = dot_nn(grad_scores, content_head)
        content_parts.append(left_factor(keys_head, grad_scores))
        turned = dot_nn(stacked_t_ref[...], grad_scores)
        turn_c, turn_s = turned[:HALF], turned[HALF:]
        lifted = jnp.concatenate(
            [turn_c * sine - turn_s * cosine, turn_c * cosine + turn_s * sine], axis=0
        ).astype(jnp.bfloat16)
        position_parts.append(left_factor(place_head, lifted))
        place_part = dot_nn(lifted, head_mask(query_position, head))
        if head == 0:
            grad_keys, grad_values, grad_place = key_part, value_part, place_part
        else:
            grad_keys += key_part
            grad_values += value_part
            grad_place += place_part
    grad_content = (content_parts[0] + content_parts[1]).T
    grad_position = (position_parts[0] + position_parts[1]).T
    grad_query_ref[0] = (grad_content + grad_position).astype(jnp.bfloat16)
    grad_key_ref[0] = grad_keys.astype(jnp.bfloat16)
    grad_value_ref[0] = grad_values.astype(jnp.bfloat16)
    sums_ref[0, 0] = jnp.concatenate(
        [
            jnp.sum(grad_content, axis=0, keepdims=True),
            jnp.sum(grad_position, axis=0, keepdims=True),
            jnp.sum(grad_values, axis=0, keepdims=True),
            jnp.zeros((5, PAIR), jnp.float32),
        ],
        axis=0,
    )

    @pl.when(pl.program_id(1) == 0)
    def _():
        grad_place_ref[...] = grad_place

    @pl.when(pl.program_id(1) != 0)
    def _():
        grad_place_ref[...] += grad_place


def clip_block(offset=0):
    return pl.BlockSpec((1, ROWS, PAIR), lambda pair, clip: (clip, 0, pair + offset))


def whole_block(shape):
    return pl.BlockSpec(shape, lambda pair, clip: (0,) * len(shape))


def pair_block(rows):
    return pl.BlockSpec((1, 1, rows, ROWS), lambda pair, clip: (clip, pair, 0, 0))


def attend_call(query_content, query_position, key_rows, value_rows, place, tables):
    clip_count = query_content.shape[0]
    sine, cosine, stacked, _ = tables
    return pl.pallas_call(
        attend_kernel,
        grid=(PAIRS, clip_count),
        in_specs=[clip_block()] * 4
        + [
            pl.BlockSpec((D, PAIR), lambda pair, clip: (0, pair)),
            whole_block((HALF, ROWS)),
            whole_block((HALF, ROWS)),
            whole_block((ROWS, D)),
        ],
        out_specs=[clip_block(), pair_block(2)],
        out_shape=[
            jax.ShapeDtypeStruct((clip_count, ROWS, D), jnp.bfloat16),
            jax.ShapeDtypeStruct((clip_count, PAIRS, 2, ROWS), jnp.float32),
        ],
        compiler_params=pltpu.CompilerParams(vmem_limit_bytes=56 << 20),
    )(query_content, query_position, key_rows, value_rows, place, sine, cosine, stacked)


def attend_back_call(
    query_content, query_position, key_rows, value_rows, grad_context, totals, place, tables
):
    clip_count = query_content.shape[0]
    sine, cosine, stacked, stacked_t = tables
    return pl.pallas_call(
        attend_back_kernel,
        grid=(PAIRS, clip_count),
        in_specs=[clip_block()] * 5
        + [
            pair_block(2),
            pl.BlockSpec((D, PAIR), lambda pair, clip: (0, pair)),
            whole_block((HALF, ROWS)),
            whole_block((HALF, ROWS)),
            whole_block((ROWS, D)),
            whole_block((D, ROWS)),
        ],
        out_specs=[clip_block()] * 3
        + [
            pl.BlockSpec((1, 1, 8, PAIR), lambda pair, clip: (clip, pair, 0, 0)),
            pl.BlockSpec((D, PAIR), lambda pair, clip: (0, pair)),
        ],
        out_shape=[jax.ShapeDtypeStruct((clip_count, ROWS, D), jnp.bfloat16)] * 3
        + [
            jax.ShapeDtypeStruct((clip_count, PAIRS, 8, PAIR), jnp.float32),
            jax.ShapeDtypeStruct((D, D), jnp.float32),
        ],
        compiler_params=pltpu.CompilerParams(vmem_limit_bytes=56 << 20),
    )(
        query_content, query_position, key_rows, value_rows, grad_context, totals, place,
        sine, cosine, stacked, stacked_t,
    )


def depthwise(gated, kernel):
    margin = (KERNEL - 1) // 2
    padded = jnp.pad(gated, ((0, 0), (margin, margin), (0, 0)))
    summed = jnp.zeros_like(gated)
    for tap_index in range(KERNEL):
        summed = summed + kernel[tap_index] * padded[:, tap_index : tap_index + ROWS, :]
    return summed


def depthwise_back(grad_out, gated, kernel):
    margin = (KERNEL - 1) // 2
    padded_grad = jnp.pad(grad_out, ((0, 0), (margin, margin), (0, 0)))
    padded_gated = jnp.pad(gated, ((0, 0), (margin, margin), (0, 0)))
    grad_gated = jnp.zeros_like(gated)
    kernel_rows = []
    for tap_index in range(KERNEL):
        begin_row = 2 * margin - tap_index
        grad_gated = (
            grad_gated + kernel[tap_index] * padded_grad[:, begin_row : begin_row + ROWS, :]
        )
        kernel_rows.append(
            jnp.sum(grad_out * padded_gated[:, tap_index : tap_index + ROWS, :], axis=(0, 1))
        )
    return (grad_gated, jnp.stack(kernel_rows))


def ffn_forward(residual, w_in, bias_in, w_out, vector_full, first_row):
    normed, unit_field, inverse = norm_forward(
        residual, vector_full[first_row], vector_full[first_row + 1]
    )
    normed = normed.astype(jnp.bfloat16)
    hidden = product(normed, w_in) + bias_in
    active = swish_act(hidden).astype(jnp.bfloat16)
    result = residual + 0.5 * (product(active, w_out) + vector_full[first_row + 2])
    return (result, (normed, unit_field, inverse, hidden, active))


def perceptron_reverse(grad_field, saved, w_in, w_out, vector_full, first_row):
    normed, unit_field, inverse, hidden, active = saved
    bisected_value = 0.5 * grad_field
    halved_low = bisected_value.astype(jnp.bfloat16)
    grad_out_weight = left_factor(active, halved_low)
    grad_active = product_right(halved_low, w_out)
    grad_hidden = grad_active * swish_slope(hidden)
    hidden_low = grad_hidden.astype(jnp.bfloat16)
    grad_in_weight = left_factor(normed, hidden_low)
    grad_normed = product_right(hidden_low, w_in)
    grad_input, grad_gain, grad_shift = norm_backward(
        grad_normed, unit_field, inverse, vector_full[first_row]
    )
    return (
        grad_field + grad_input,
        (
            grad_in_weight,
            jnp.sum(grad_hidden, axis=0),
            grad_out_weight,
            grad_gain,
            grad_shift,
            jnp.sum(bisected_value, axis=0),
        ),
    )


def valid_rows(clip_count):
    token = lax.broadcasted_iota(jnp.int32, (clip_count, ROWS, 1), 1)
    return token < CLIP_LEN


def attend_forward(residual, w_triple, w_place, w_attend, vector_full, tables):
    row_count = residual.shape[0]
    clip_count = row_count // ROWS
    normed, unit_field, inverse = norm_forward(
        residual, vector_full[attend_gain], vector_full[attend_shift]
    )
    normed = normed.astype(jnp.bfloat16)
    triple = product(normed, w_triple)
    queries = triple[:, :D] + vector_full[query_bias]
    query_content = (queries + vector_full[content_bias]).astype(jnp.bfloat16)
    query_position = (queries + vector_full[position_bias]).astype(jnp.bfloat16)
    key_rows = triple[:, D : 2 * D].astype(jnp.bfloat16)
    value_rows = (triple[:, 2 * D :] + vector_full[value_bias]).astype(jnp.bfloat16)
    place = jnp.concatenate([w_place[0::2], w_place[1::2]], axis=0)
    packed = tuple(
        (
            member.reshape(clip_count, ROWS, D)
            for member in (query_content, query_position, key_rows, value_rows)
        )
    )
    context, totals = attend_call(*packed, place, tables)
    context = context.reshape(row_count, D)
    result = residual + product(context, w_attend) + vector_full[attend_out]
    return (result, (normed, unit_field, inverse, packed, place, context, totals))


def attend_backward(grad_field, saved, w_triple, w_attend, vector_full, tables):
    normed, unit_field, inverse, packed, place, context, totals = saved
    row_count = grad_field.shape[0]
    clip_count = row_count // ROWS
    grad_low = grad_field.astype(jnp.bfloat16)
    grad_attend = left_factor(context, grad_low)
    grad_context = (
        product_right(grad_low, w_attend).astype(jnp.bfloat16).reshape(clip_count, ROWS, D)
    )
    grad_queries, grad_keys, grad_values, sums, grad_place = attend_back_call(
        *packed, grad_context, totals, place, tables
    )
    grad_place_weight = jnp.stack([grad_place[:HALF], grad_place[HALF:]], axis=1).reshape(D, D)
    grad_triple = jnp.concatenate(
        [member.reshape(row_count, D) for member in (grad_queries, grad_keys, grad_values)],
        axis=1,
    )
    grad_triple_weight = left_factor(normed, grad_triple)
    grad_normed = product_right(grad_triple, w_triple)
    grad_input, grad_gain, grad_shift = norm_backward(
        grad_normed, unit_field, inverse, vector_full[attend_gain]
    )
    sums = jnp.sum(sums, axis=0).transpose(1, 0, 2).reshape(8, D)
    vector_rows = (
        grad_gain,
        grad_shift,
        sums[0] + sums[1],
        sums[2],
        jnp.sum(grad_field, axis=0),
        sums[0],
        sums[1],
    )
    return (
        grad_field + grad_input,
        grad_triple_weight,
        grad_place_weight,
        grad_attend,
        vector_rows,
    )


def conv_forward(residual, w_glu, w_point, vector_full):
    row_count = residual.shape[0]
    clip_count = row_count // ROWS
    normed, unit_field, inverse = norm_forward(
        residual, vector_full[conv_gain], vector_full[conv_shift]
    )
    normed = normed.astype(jnp.bfloat16)
    glu_pre = product(normed, w_glu) + jnp.concatenate(
        [vector_full[glu_value], vector_full[glu_gate]]
    )
    value_half = glu_pre[:, :D]
    gate_logistic = jax.nn.sigmoid(glu_pre[:, D:])
    valid = valid_rows(clip_count)
    gated = jnp.where(valid, (value_half * gate_logistic).reshape(clip_count, ROWS, D), 0.0)
    kernel = vector_full[kernel_start : kernel_start + KERNEL]
    depth_out = depthwise(gated, kernel)
    local_count = float(clip_count * CLIP_LEN)
    device_count = lax.axis_size("rep") * lax.axis_size("shard")
    token_count = device_count * local_count
    local_mean = jnp.sum(jnp.where(valid, depth_out, 0.0), axis=(0, 1)) / local_count
    local_square = jnp.sum(
        jnp.where(valid, (depth_out - local_mean) ** 2, 0.0), axis=(0, 1)
    )
    both = lax.all_gather(jnp.stack([local_mean, local_square]), ("rep", "shard"))
    mean_depth = jnp.mean(both[:, 0], axis=0)
    between = jnp.sum((both[:, 0] - mean_depth) ** 2, axis=0) * local_count
    var_depth = (jnp.sum(both[:, 1], axis=0) + between) / token_count
    centered = depth_out - mean_depth
    inverse_batch = lax.rsqrt(var_depth + norm_eps)
    unit_batch = centered * inverse_batch
    normed_batch = unit_batch * vector_full[batch_gain] + vector_full[batch_shift]
    active = swish_act(normed_batch).astype(jnp.bfloat16).reshape(row_count, D)
    result = residual + product(active, w_point) + vector_full[conv_out]
    return (
        result,
        (
            normed,
            unit_field,
            inverse,
            value_half,
            gate_logistic,
            gated,
            unit_batch,
            inverse_batch,
            normed_batch,
            active,
            token_count,
        ),
    )


def conv_backward(grad_field, saved, w_glu, w_point, vector_full):
    (
        normed,
        unit_field,
        inverse,
        value_half,
        gate_logistic,
        gated,
        unit_batch,
        inverse_batch,
        normed_batch,
        active,
        token_count,
    ) = saved
    row_count = grad_field.shape[0]
    clip_count = row_count // ROWS
    grad_low = grad_field.astype(jnp.bfloat16)
    grad_point = left_factor(active, grad_low)
    grad_active = product_right(grad_low, w_point).reshape(clip_count, ROWS, D)
    grad_norm = grad_active * swish_slope(normed_batch)
    local_shift = jnp.sum(grad_norm, axis=(0, 1))
    local_gain = jnp.sum(grad_norm * unit_batch, axis=(0, 1))
    total_shift, overall_multiplier = lax.psum(
        jnp.stack([local_shift, local_gain]), ("rep", "shard")
    )
    valid = valid_rows(clip_count)
    grad_depth = (
        vector_full[batch_gain]
        * inverse_batch
        * (grad_norm - total_shift / token_count - unit_batch * (overall_multiplier / token_count))
    )
    grad_depth = jnp.where(valid, grad_depth, 0.0)
    kernel = vector_full[kernel_start : kernel_start + KERNEL]
    grad_gated, grad_kernel = depthwise_back(grad_depth, gated, kernel)
    grad_gated = jnp.where(valid, grad_gated, 0.0).reshape(row_count, D)
    grad_value = grad_gated * gate_logistic
    grad_gate = grad_gated * value_half * gate_logistic * (1.0 - gate_logistic)
    glu_low = jnp.concatenate([grad_value, grad_gate], axis=1).astype(jnp.bfloat16)
    grad_glu_weight = left_factor(normed, glu_low)
    grad_normed = product_right(glu_low, w_glu)
    grad_input, grad_gain, grad_shift = norm_backward(
        grad_normed, unit_field, inverse, vector_full[conv_gain]
    )
    return (
        grad_field + grad_input,
        (
            grad_glu_weight,
            grad_point,
            grad_gain,
            grad_shift,
            jnp.sum(grad_value, axis=0),
            jnp.sum(grad_gate, axis=0),
            jnp.sum(grad_field, axis=0),
            local_gain,
            local_shift,
            grad_kernel,
        ),
    )


def adam_step(weight, gradient, first, second, count_steps):
    first_new = beta_first * first + (1.0 - beta_first) * gradient
    second_new = beta_second * second + (1.0 - beta_second) * gradient * gradient
    first_fix = 1.0 - jnp.power(beta_first, count_steps)
    second_fix = 1.0 - jnp.power(beta_second, count_steps)
    update = -learn_rate * (
        first_new / first_fix / (jnp.sqrt(second_new / second_fix) + adam_eps)
        + weight_decay * weight
    )
    return (first_new, second_new, update)


def shards(
    inputs,
    cotangent,
    row_weights,
    down_weights,
    hidden_bias,
    vectors,
    row_first,
    down_first,
    hidden_first,
    vector_first,
    row_second,
    down_second,
    hidden_second,
    vector_second,
    step_number,
):
    clip_count = inputs.shape[0]
    row_count = clip_count * ROWS
    shard_count = lax.axis_size("shard")
    offset_cols = 2 * FF
    hidden_cols = FF // shard_count
    vector_cols = D // shard_count
    hidden_lines = 2 * hidden_cols // vector_cols
    row_total = vectors.shape[0]

    def gather(piece):
        return lax.all_gather(piece, "shard", axis=0, tiled=True)

    small = lax.all_gather(
        jnp.concatenate([vectors, hidden_bias.reshape(hidden_lines, vector_cols)], axis=0), "shard"
    ).astype(jnp.float32)
    vector_full = small[:, :row_total].transpose(1, 0, 2).reshape(row_total, D)
    hidden_full = (
        small[:, row_total:].reshape(shard_count, 2, hidden_cols).transpose(1, 0, 2).reshape(2, FF)
    )
    w_front = gather(row_weights[:, :FF])
    down_front = gather(down_weights[0])
    w_rest = gather(row_weights[:, offset_cols:])
    w_back = gather(row_weights[:, FF:offset_cols])
    down_back = gather(down_weights[1])
    w_triple = w_rest[:, : 3 * D]
    w_place = w_rest[:, 3 * D : 4 * D]
    w_glu = w_rest[:, 4 * D : 6 * D]
    w_attend = w_rest[:, 6 * D : 7 * D]
    w_point = w_rest[:, 7 * D :]
    tables = angle_tables()
    extra = ((0, 0), (0, ROWS - CLIP_LEN), (0, 0))
    residual = jnp.pad(inputs, extra).reshape(row_count, D).astype(jnp.float32)
    cotangent_rows = jnp.pad(cotangent, extra).reshape(row_count, D)
    front, stored_leading_block = ffn_forward(
        residual, w_front, hidden_full[0], down_front, vector_full, front_gain
    )
    attended, saved_attend = attend_forward(
        front, w_triple, w_place, w_attend, vector_full, tables
    )
    convolved, saved_conv = conv_forward(attended, w_glu, w_point, vector_full)
    back_field, saved_back = ffn_forward(
        convolved, w_back, hidden_full[1], down_back, vector_full, back_gain
    )
    outputs, unit_final, inverse_final = norm_forward(
        back_field, vector_full[final_gain], vector_full[final_shift]
    )
    grad_back, final_gain_grad, final_shift_grad = norm_backward(
        cotangent_rows, unit_final, inverse_final, vector_full[final_gain]
    )
    grad_conv, back_grads = perceptron_reverse(
        grad_back, saved_back, w_back, down_back, vector_full, back_gain
    )
    grad_attended, conv_grads = conv_backward(grad_conv, saved_conv, w_glu, w_point, vector_full)
    grad_front, triple_grad, place_grad, attend_grad, attend_rows = attend_backward(
        grad_attended, saved_attend, w_triple, w_attend, vector_full, tables
    )
    grad_input, front_grads = perceptron_reverse(
        grad_front, stored_leading_block, w_front, down_front, vector_full, front_gain
    )
    hidden_grad = jnp.stack([front_grads[1], back_grads[1]])
    vector_rows = (
        [front_grads[3], front_grads[4], front_grads[5]]
        + list(attend_rows)
        + list(conv_grads[2:9])
        + [back_grads[3], back_grads[4], back_grads[5], final_gain_grad, final_shift_grad]
    )
    vector_grad = jnp.concatenate([jnp.stack(vector_rows), conv_grads[9]], axis=0)

    def reduce(piece):
        piece = lax.psum_scatter(
            piece.astype(jnp.bfloat16), "shard", scatter_dimension=0, tiled=True
        )
        return lax.psum(piece, "rep").astype(jnp.float32)

    back_sum = reduce(back_grads[0])
    down_back_sum = reduce(back_grads[2])
    conv_sum = reduce(jnp.concatenate([conv_grads[0], attend_grad, conv_grads[1]], axis=1))
    attend_sum = reduce(jnp.concatenate([triple_grad, place_grad], axis=1))
    down_front_sum = reduce(front_grads[2])
    front_sum = reduce(front_grads[0])
    small_grad = jnp.concatenate(
        [
            vector_grad.reshape(row_total, shard_count, vector_cols).transpose(1, 0, 2),
            hidden_grad.reshape(2, shard_count, hidden_cols)
            .transpose(1, 0, 2)
            .reshape(shard_count, hidden_lines, vector_cols),
        ],
        axis=1,
    )
    small_sum = lax.psum(small_grad, ("rep", "shard"))[lax.axis_index("shard")]
    owned_grads = (
        jnp.concatenate([front_sum, back_sum, attend_sum, conv_sum], axis=1),
        jnp.stack([down_front_sum, down_back_sum]),
        small_sum[row_total:].reshape(2, hidden_cols),
        small_sum[:row_total],
    )
    count_steps = step_number[0].astype(jnp.float32)
    row_new = adam_step(
        row_weights.astype(jnp.float32), owned_grads[0], row_first, row_second, count_steps
    )
    down_new = adam_step(
        down_weights.astype(jnp.float32), owned_grads[1], down_first, down_second, count_steps
    )
    latent_matrix_revised = adam_step(
        hidden_bias.astype(jnp.float32), owned_grads[2], hidden_first, hidden_second, count_steps
    )
    array_revised = adam_step(
        vectors.astype(jnp.float32), owned_grads[3], vector_first, vector_second, count_steps
    )
    return (
        outputs.reshape(clip_count, ROWS, D)[:, :CLIP_LEN],
        grad_input.reshape(clip_count, ROWS, D)[:, :CLIP_LEN],
        owned_grads[0],
        owned_grads[1],
        owned_grads[2],
        owned_grads[3],
        row_new[0],
        down_new[0],
        latent_matrix_revised[0],
        array_revised[0],
        row_new[1],
        down_new[1],
        latent_matrix_revised[1],
        array_revised[1],
        row_new[2],
        down_new[2],
        latent_matrix_revised[2],
        array_revised[2],
    )


def solution(mesh):
    in_specs = (
        P(("rep", "shard"), None, None),
        P(("rep", "shard"), None, None),
        P("shard", None),
        P(None, "shard", None),
        P(None, "shard"),
        P(None, "shard"),
        P("shard", None),
        P(None, "shard", None),
        P(None, "shard"),
        P(None, "shard"),
        P("shard", None),
        P(None, "shard", None),
        P(None, "shard"),
        P(None, "shard"),
        P(),
    )
    out_specs = (
        P(("rep", "shard"), None, None),
        P(("rep", "shard"), None, None),
        P("shard", None),
        P(None, "shard", None),
        P(None, "shard"),
        P(None, "shard"),
        P("shard", None),
        P(None, "shard", None),
        P(None, "shard"),
        P(None, "shard"),
        P("shard", None),
        P(None, "shard", None),
        P(None, "shard"),
        P(None, "shard"),
        P("shard", None),
        P(None, "shard", None),
        P(None, "shard"),
        P(None, "shard"),
    )
    return jax.shard_map(shards, mesh=mesh, in_specs=in_specs, out_specs=out_specs, check_vma=False)
```

profile of v0, /device:TPU:0, one launch (start us, length us, event | category | flops | bytes accessed | tf_op | source)
XLA Modules:
  0.0 1121.2 jit_solution(6644612947474686623)
XLA Ops:
  23.5 33.2 %all-gather.4 = bf16[8,61,64]{2,1,0:T(8,128)(2,1)S(1)} all-gather(bf16[1,61,64]{2,1,0:T(8,128)(2,1)S(1)} %maximum_bitcast_fusion), channel_id=2, replica_groups=mesh['rep'=4,'shard'=8] {'shard'}, dimensions={0}, use_global_device_ids=true | all-gather | bytes 70272 | tf_op jit(solution)/shard_map/all_gather | solution.py:581
  155.8 10.9 multiply_convert_fusion.1
  175.4 13.1 %all-gather.14.cloned.1.call-done = bf16[512,4096]{1,0:T(8,128)(2,1)} async-done(((bf16[64,4096]{1,0:T(8,128)(2,1)}), bf16[512,4096]{1,0:T(8,128)(2,1)}) %all-gather.14.cloned.1.call-update) | async-done | bytes 4194320 | tf_op jit(solution)/shard_map/all_gather | solution.py:579
  201.1 36.3 %shard_map.286 = (bf16[2,768,512]{2,1,0:T(8,128)(2,1)}, f32[2,4,2,768]{3,2,1,0:T(2,128)}) custom-call(bf16[2,768,512]{2,1,0:T(8,128)(2,1)} %bitcast.138, bf16[2,768,512]{2,1,0:T(8,128)(2,1)} %bitcast.136, bf16[2,768,512]{2,1,0:T(8,128)(2,1)} %bitcast.142, bf16[2,768,512]{2,1,0:T(8,128)(2,1)} %bitcast.140, bf16[512,512]{1,0:T(8,128)(2,1)} %pad_maximum_fusion.10.place_ref, ...), custom_call_target="tpu_custom_call" | custom-call | tf_op jit(solution)/shard_map/pallas_call | solution.py:241
  248.0 15.0 %select_reduce_fusion.1 = (f32[512]{0:T(512)S(1)}, f32[2,768,512]{2,1,0:T(8,128)S(1)}) fusion(pred[768]{0:T(1024)(128)(4,1)S(1)} %copy-done.59, f32[512]{0:T(512)S(1)} %copy-done.87, f32[512]{0:T(512)S(1)} %copy-done.86, f32[512]{0:T(512)S(1)} %copy-done.85, f32[512]{0:T(512)S(1)} %copy-done.84, f32[512]{0:T(512)S(1)} %copy-done.83, f32[512]{0:T(512)S(1)} %copy-done.82, ...), kind=kLoop, calls=%fused_computation.142 | loop fusion | flops 49544704 | bytes 6357760 | tf_op jit(solution)/shard_map/reduce_sum | solution.py:448
  263.5 66.8 %all-gather.5 = f32[32,2,512]{2,1,0:T(2,128)S(1)} all-gather(f32[1,2,512]{2,1,0:T(2,128)S(1)} %maximum_bitcast_fusion.2), channel_id=4, replica_groups=mesh['rep'=4,'shard'=8] {'rep','shard'}, dimensions={0}, use_global_device_ids=true | all-gather | bytes 135168 | tf_op jit(solution)/shard_map/all_gather | solution.py:452
  336.4 11.2 %multiply_convert_fusion = (bf16[1536,2048]{1,0:T(8,128)(2,1)}, f32[1536,2048]{1,0:T(8,128)}) fusion(f32[2048]{0:T(1024)S(1)} %bitcast.168, bf16[512,2048]{1,0:T(8,128)(2,1)} %all-gather.16.cloned.1.call-done, f32[1536,512]{1,0:T(8,128)} %copy-done.14, f32[512]{0:T(512)S(1)} %copy-done.121, f32[512]{0:T(512)S(1)} %copy-done.100, ...), kind=kOutput, calls=%fused_computation.2 | convolution fusion | flops 3244032000 | bytes 24141824 | tf_op jit(solution)/shard_map/dot_general | solution.py:50
  347.6 8.0 fusion.109
  369.6 11.2 fusion.110
  392.9 37.3 %psum.56 = f32[2,512]{1,0:T(2,128)S(1)} all-reduce(f32[2,512]{1,0:T(2,128)S(1)} %pad_maximum_fusion.14), channel_id=1, replica_groups=mesh['rep'=4,'shard'=8] {'rep','shard'}, use_global_device_ids=true, to_apply=%region_21.22 | all-reduce | flops 1024 | bytes 8192 | tf_op jit(solution)/shard_map/psum | solution.py:502
  430.2 28.6 %multiply_reduce_fusion = (f32[512]{0:T(512)}, f32[512]{0:T(512)S(1)}, f32[512]{0:T(512)S(1)}, f32[512]{0:T(512)S(1)}, f32[512]{0:T(512)S(1)}, /*index=5*/f32[51...) fusion(f32[2,768,512]{2,1,0:T(8,128)} %copy-done, ...), kind=kLoop, calls=%fused_computation.37 | loop fusion | flops 33807360 | bytes 12630784 | tf_op jit(solution)/shard_map/reduce_sum | solution.py:315
  458.8 14.8 %add_select_fusion = f32[2,768,512]{2,1,0:T(8,128)S(1)} fusion(f32[2,768,512]{2,1,0:T(8,128)S(1)} %get-tuple-element.166, f32[512]{0:T(512)S(1)} %copy-done.87, f32[512]{0:T(512)S(1)} %copy-done.86, f32[512]{0:T(512)S(1)} %copy-done.85, f32[512]{0:T(512)S(1)} %copy-done.84, f32[512]{0:T(512)S(1)} %copy-done.83, f32[512]{0:T(512)S(1)} %copy-done.82, ...), kind=kLoop, calls=%fused_computation.82 | loop fusion | flops 48758784 | bytes 6355712 | tf_op jit(solution)/shard_map/jit(_where)/select_n | solution.py:514
  489.1 68.8 %shard_map.287 = (bf16[2,768,512]{2,1,0:T(8,128)(2,1)}, bf16[2,768,512]{2,1,0:T(8,128)(2,1)}, bf16[2,768,512]{2,1,0:T(8,128)(2,1)}, f32[2,4,8,128]{3,2,1,0:T(8,128)}, f32[512,512]{1,0:T(8,128)}) custom-call(bf16[2,768,512]{2,1,0:T(8,128)(2,1)} %bitcast.139, bf16[2,768,512]{2,1,0:T(8,128)(2,1)} %bitcast.137, bf16[2,768,512]{2,1,0:T(8,128)(2,1)} %bitcast.143, ...), custom_call_target="tpu_custom_call" | custom-call | tf_op jit(solution)/shard_map/pallas_call | solution.py:265
  567.5 7.9 convolution_convert_fusion.2
  575.4 8.8 fusion.47
  597.8 11.6 %fusion.111 = (f32[2048]{0:T(1024)S(1)}, bf16[1536,2048]{1,0:T(8,128)(2,1)S(1)}) fusion(f32[1536,2048]{1,0:T(8,128)} %get-tuple-element.204, f32[2048]{0:T(1024)S(1)} %bitcast.166, bf16[1,2048,512]{2,1,0:T(8,128)(2,1)} %all-gather.18.cloned.1.call-done, f32[1536,512]{1,0:T(8,128)} %copy-done.23), kind=kOutput, calls=%fused_computation.408 | convolution fusion | flops 3257399296 | bytes 24133632 | tf_op jit(solution)/shard_map/dot_general | solution.py:60
  627.4 8.4 fusion.50
  635.8 6.9 multiply_reduce_fusion.18
  653.1 62.9 %reduce-scatter.9.cloned.1.call-done = bf16[64,2048]{1,0:T(8,128)(2,1)} async-done(((bf16[512,2048]{1,0:T(8,128)(2,1)}), bf16[64,2048]{1,0:T(8,128)(2,1)}) %reduce-scatter.9.cloned.1.call-update) | async-done | bytes 262160 | tf_op jit(solution)/shard_map/reduce_scatter | solution.py:638
  716.0 71.6 %reduce-scatter.11.cloned.1.call-done = bf16[64,2048]{1,0:T(8,128)(2,1)} async-done(((bf16[512,2048]{1,0:T(8,128)(2,1)}), bf16[64,2048]{1,0:T(8,128)(2,1)}) %reduce-scatter.11.cloned.1.call-update) | async-done | bytes 262160 | tf_op jit(solution)/shard_map/reduce_scatter | solution.py:638
  787.6 71.3 %reduce-scatter.13.cloned.1.call-done = bf16[64,2048]{1,0:T(8,128)(2,1)} async-done(((bf16[512,2048]{1,0:T(8,128)(2,1)}), bf16[64,2048]{1,0:T(8,128)(2,1)}) %reduce-scatter.13.cloned.1.call-update) | async-done | bytes 262160 | tf_op jit(solution)/shard_map/reduce_scatter | solution.py:638
  858.9 71.5 %reduce-scatter.7.cloned.1.call-done = bf16[64,2048]{1,0:T(8,128)(2,1)} async-done(((bf16[512,2048]{1,0:T(8,128)(2,1)}), bf16[64,2048]{1,0:T(8,128)(2,1)}) %reduce-scatter.7.cloned.1.call-update) | async-done | bytes 262160 | tf_op jit(solution)/shard_map/reduce_scatter | solution.py:638
  942.6 118.6 %all-reduce.8.cloned.1.call-done = f32[8,61,64]{2,0,1:T(8,128)} async-done(((f32[8,61,64]{2,0,1:T(8,128)}), f32[8,61,64]{2,0,1:T(8,128)}) %all-reduce.8.cloned.1.call-update) | async-done | bytes 124944 | tf_op jit(solution)/shard_map/psum | solution.py:658
  1064.3 42.4 %all-reduce.10.cloned.1.call-done = (bf16[64,2048]{1,0:T(8,128)(2,1)}, bf16[64,2048]{1,0:T(8,128)(2,1)}, bf16[64,2048]{1,0:T(8,128)(2,1)}, bf16[64,2048]{1,0:T(8...) async-done(((bf16[64,2048]{1,0:T(8,128)(2,1)}, bf16[64,2048]{1,0:T(8,128)(2,1)}, bf16[64,2048]{1,0:T(8,128)(2,1)}, bf16[64,2048]{1,0:T(8,128)(2,1)}, ...) | async-done | bytes 1572880 | tf_op jit(solution)/shard_map/psum | solution.py:641
  (580 shorter events, 267.1 us)
Async XLA Ops:
  7.2 148.6 %all-gather.12.cloned.1.call-start = ((), (), s32[]{:S(2)}) async-start(), calls=%async_computation.6 | async-start | bytes 2359296 | tf_op jit(solution)/shard_map/all_gather | solution.py:579
  9.2 157.5 %all-gather.18.cloned.1.call-start = ((), (), s32[]{:S(2)}) async-start(), calls=%async_computation.16 | async-start | bytes 2359296 | tf_op jit(solution)/shard_map/all_gather | solution.py:579
  11.2 177.3 %all-gather.14.cloned.1.call-start = ((), (), s32[]{:S(2)}) async-start(), calls=%async_computation.7 | async-start | bytes 4718592 | tf_op jit(solution)/shard_map/all_gather | solution.py:579
  13.1 323.2 %all-gather.16.cloned.1.call-start = ((), (), s32[]{:S(2)}) async-start(), calls=%async_computation.8 | async-start | bytes 2359296 | tf_op jit(solution)/shard_map/all_gather | solution.py:579
  13.7 333.9 %all-gather.20.cloned.1.call-start = ((), (), s32[]{:S(2)}) async-start(), calls=%async_computation.17 | async-start | bytes 2359296 | tf_op jit(solution)/shard_map/all_gather | solution.py:579
  14.3 638.8 %reduce-scatter.17.cloned.1.call-start = ((), (), s32[]{:S(2)}) async-start(), calls=%async_computation.14 | async-start | bytes 2359296 | tf_op jit(solution)/shard_map/reduce_scatter | solution.py:638
  67.4 99.3 %copy-start.4 = (f32[2,768,512]{2,1,0:T(8,128)}, f32[2,768,512]{2,1,0:T(8,128)S(1)}, u32[]{:S(2)}) copy-start(f32[2,768,512]{2,1,0:T(8,128)S(1)} %copy.93) | copy-start | bytes 9437188
  478.4 174.6 %reduce-scatter.15.cloned.1.call-start = ((), (), s32[]{:S(2)}) async-start(), calls=%async_computation.13 | async-start | bytes 2359296 | tf_op jit(solution)/shard_map/reduce_scatter | solution.py:638
  575.4 140.6 %reduce-scatter.9.cloned.1.call-start = ((), (), s32[]{:S(2)}) async-start(), calls=%async_computation.10 | async-start | bytes 2359296 | tf_op jit(solution)/shard_map/reduce_scatter | solution.py:638
  584.2 203.4 %reduce-scatter.11.cloned.1.call-start = ((), (), s32[]{:S(2)}) async-start(), calls=%async_computation.11 | async-start | bytes 2359296 | tf_op jit(solution)/shard_map/reduce_scatter | solution.py:638
  597.7 261.2 %reduce-scatter.13.cloned.1.call-start = ((), (), s32[]{:S(2)}) async-start(), calls=%async_computation.12 | async-start | bytes 2359296 | tf_op jit(solution)/shard_map/reduce_scatter | solution.py:638
  625.7 304.6 %reduce-scatter.7.cloned.1.call-start = ((), (), s32[]{:S(2)}) async-start(), calls=%async_computation.9 | async-start | bytes 2359296 | tf_op jit(solution)/shard_map/reduce_scatter | solution.py:638
  642.7 287.6 %copy-start.6 = (f32[2,768,512]{2,1,0:T(8,128)S(1)}, f32[2,768,512]{2,1,0:T(8,128)}, u32[]{:S(2)}) copy-start(f32[2,768,512]{2,1,0:T(8,128)} %copy-done.4) | copy-start | bytes 9437188
  642.8 418.4 %all-reduce.8.cloned.1.call-start = ((), (), s32[]{:S(2)}) async-start(), calls=%async_computation.15 | async-start | bytes 499712 | tf_op jit(solution)/shard_map/psum | solution.py:658
  652.3 454.4 %all-reduce.10.cloned.1.call-start = ((), (), s32[]{:S(2)}) async-start(), calls=%async_computation.18 | async-start | bytes 3145728 | tf_op jit(solution)/shard_map/psum | solution.py:641
  938.5 124.5 %copy-start.114 = (bf16[2,256]{1,0:T(2,128)(2,1)S(1)}, bf16[2,256]{1,0:T(2,128)(2,1)}, u32[]{:S(2)}) copy-start(bf16[2,256]{1,0:T(2,128)(2,1)} %param.19) | copy-start | bytes 3076
  938.5 124.5 %copy-start.115 = (f32[2,256]{1,0:T(2,128)S(1)}, f32[2,256]{1,0:T(2,128)}, u32[]{:S(2)}) copy-start(f32[2,256]{1,0:T(2,128)} %param.27) | copy-start | bytes 6148
  938.5 124.5 %copy-start.116 = (f32[2,256]{1,0:T(2,128)S(1)}, f32[2,256]{1,0:T(2,128)}, u32[]{:S(2)}) copy-start(f32[2,256]{1,0:T(2,128)} %param.23) | copy-start | bytes 6148
  938.5 125.1 %copy-start.50 = (bf16[53,64]{1,0:T(8,128)(2,1)S(1)}, bf16[53,64]{1,0:T(8,128)(2,1)}, u32[]{:S(2)}) copy-start(bf16[53,64]{1,0:T(8,128)(2,1)} %param.20) | copy-start | bytes 20356
  938.6 125.1 %copy-start.57 = (f32[53,64]{1,0:T(8,128)S(1)}, f32[53,64]{1,0:T(8,128)}, u32[]{:S(2)}) copy-start(f32[53,64]{1,0:T(8,128)} %param.28) | copy-start | bytes 40708
  938.6 125.1 %copy-start.58 = (f32[53,64]{1,0:T(8,128)S(1)}, f32[53,64]{1,0:T(8,128)}, u32[]{:S(2)}) copy-start(f32[53,64]{1,0:T(8,128)} %param.24) | copy-start | bytes 40708
  938.6 168.1 %copy-start.31 = (bf16[2,256,512]{2,1,0:T(8,128)(2,1)S(1)}, bf16[2,256,512]{2,1,0:T(8,128)(2,1)}, u32[]{:S(2)}) copy-start(bf16[2,256,512]{2,1,0:T(8,128)(2,1)} %param.18) | copy-start | bytes 1572868
  938.6 168.1 %copy-start.37 = (f32[2,256,512]{2,1,0:T(8,128)S(1)}, f32[2,256,512]{2,1,0:T(8,128)}, u32[]{:S(2)}) copy-start(f32[2,256,512]{2,1,0:T(8,128)} %param.26) | copy-start | bytes 3145732
  938.6 168.1 %copy-start.38 = (f32[2,256,512]{2,1,0:T(8,128)S(1)}, f32[2,256,512]{2,1,0:T(8,128)}, u32[]{:S(2)}) copy-start(f32[2,256,512]{2,1,0:T(8,128)} %param.22) | copy-start | bytes 3145732
  (119 other events, 1334.8 us)
Sparse Core Ops, SparseCore 0:
  10.7 53.0 all-gather.11
  66.5 47.9 all-gather.17
  117.2 71.3 all-gather.13
  191.1 47.6 all-gather.15
  241.3 48.2 all-gather.19
  478.6 68.8 reduce-scatter.16
  575.5 68.8 reduce-scatter.14
  648.5 67.4 reduce-scatter.8
  720.1 67.4 reduce-scatter.10
  791.5 67.2 reduce-scatter.12
  863.0 67.3 reduce-scatter.6
  936.3 124.8 all-reduce.7
  1064.0 42.6 all-reduce.9
where the time goes:
time: 1130 us; the launch traced here: 1120 us
  waiting for transfers between devices  453 us (40%)
  matrix products  145 us (13%)
  blocking collectives  137 us (12%)
  local copies, waits for them, and re-layouts  135 us (12%)
  other arithmetic  128 us (11%)
  Pallas kernels  105 us (9%)
  between operations  17 us (2%)
    reduce_scatter x6, waiting for transfers between devices, reduce(): lax.psum_scatter(piece.astype(jnp.bfloat16), 'shard', scatter_dimension=0...  277 us
    psum x1, waiting for transfers between devices, shards(): small_sum = lax.psum(small_grad, ('rep', 'shard'))[lax.axis_index('shard')]  119 us
    pallas_call x1, Pallas kernels, attend_back_call(): pl.pallas_call(attend_back_kernel, grid=(PAIRS, clip_count), in_specs=[cl...  68.8 us
    all_gather x1, blocking collectives, conv_forward(): lax.all_gather(jnp.stack([local_mean, local_square]), ('rep', 'shard'))  66.8 us
    dot_general x8, matrix products, product_right(): lax.dot_general(left, right, (((1,), (1,)), ((), ())), preferred_element_...  52.3 us
    dot_general x8, matrix products, product(): return jnp.dot(left, right, preferred_element_type=jnp.float32)  50.3 us
    dot_general x8, matrix products, left_factor(): lax.dot_general(left, right, (((0,), (0,)), ((), ())), preferred_element_...  42.5 us
    psum x1, waiting for transfers between devices, reduce(): return lax.psum(piece, 'rep').astype(jnp.float32)  42.4 us
  transfers between devices with their start and end apart: 13, of which 7 were waited for; matrix products, arithmetic and copies ran while one was open for 26% of the time, Pallas kernels for 9%

commit v1 on v0

--- a/solution.py
+++ b/solution.py
@@ -17,6 +17,8 @@
 HALF = D // 2
 PAIR = 2 * HEAD
 PAIRS = HEADS // 2
+LANES = 128
+MARGIN = 16
 
 
 norm_eps = 1e-05
@@ -44,6 +46,14 @@
 final_gain = 20
 final_shift = 21
 kernel_start = 22
+
+
+class Lines:
+    def __init__(self, whole):
+        self.whole = whole
+
+    def __getitem__(self, line):
+        return self.whole[line : line + 1]
 
 
 def product(left, right):
@@ -291,30 +301,205 @@
     )
 
 
-def depthwise(gated, kernel):
-    margin = (KERNEL - 1) // 2
-    padded = jnp.pad(gated, ((0, 0), (margin, margin), (0, 0)))
-    summed = jnp.zeros_like(gated)
-    for tap_index in range(KERNEL):
-        summed = summed + kernel[tap_index] * padded[:, tap_index : tap_index + ROWS, :]
-    return summed
-
-
-def depthwise_back(grad_out, gated, kernel):
-    margin = (KERNEL - 1) // 2
-    padded_grad = jnp.pad(grad_out, ((0, 0), (margin, margin), (0, 0)))
-    padded_gated = jnp.pad(gated, ((0, 0), (margin, margin), (0, 0)))
-    grad_gated = jnp.zeros_like(gated)
-    kernel_rows = []
-    for tap_index in range(KERNEL):
-        begin_row = 2 * margin - tap_index
-        grad_gated = (
-            grad_gated + kernel[tap_index] * padded_grad[:, begin_row : begin_row + ROWS, :]
+def fill_margins(buffer, field):
+    buffer[0:MARGIN, :] = jnp.zeros((MARGIN, LANES), jnp.float32)
+    buffer[MARGIN : MARGIN + ROWS, :] = field
+    buffer[MARGIN + ROWS :, :] = jnp.zeros((MARGIN, LANES), jnp.float32)
+
+
+def slide(buffer, lines_ref, reverse, store):
+    for begin in range(0, ROWS, LANES):
+        summed = jnp.zeros((LANES, LANES), jnp.float32)
+        for phase in range(8):
+            span = buffer[begin + phase : begin + phase + LANES + 24, :]
+            for block in range(4):
+                tap = 8 * block + phase - 1
+                if tap < 0:
+                    continue
+                line = kernel_start + (KERNEL - 1 - tap if reverse else tap)
+                summed += lines_ref[line : line + 1, :] * span[8 * block : 8 * block + LANES]
+        store(begin, summed)
+
+
+def row_valid(begin):
+    return lax.broadcasted_iota(jnp.int32, (LANES, LANES), 0) + begin < CLIP_LEN
+
+
+def depthwise_kernel(gated_ref, lines_ref, depth_ref, stats_ref, buffer):
+    fill_margins(buffer, gated_ref[0])
+
+    def store(begin, summed):
+        if begin + LANES > CLIP_LEN:
+            summed = jnp.where(row_valid(begin), summed, 0.0)
+        depth_ref[0, begin : begin + LANES, :] = summed
+
+    slide(buffer, lines_ref, False, store)
+    depth = depth_ref[0]
+    mean = jnp.sum(depth, axis=0, keepdims=True) / CLIP_LEN
+    token = lax.broadcasted_iota(jnp.int32, depth.shape, 0)
+    centered = jnp.where(token < CLIP_LEN, depth - mean, 0.0)
+    square = jnp.sum(centered * centered, axis=0, keepdims=True)
+    stats_ref[0] = jnp.concatenate([mean, square, jnp.zeros((6, LANES), jnp.float32)], axis=0)
+
+
+def depthwise_back_kernel(grad_ref, gated_ref, lines_ref, out_ref, taps_ref, buffer):
+    fill_margins(buffer, grad_ref[0])
+
+    def store(begin, summed):
+        if begin + LANES > CLIP_LEN:
+            summed = jnp.where(row_valid(begin), summed, 0.0)
+        out_ref[0, begin : begin + LANES, :] = summed
+
+    slide(buffer, lines_ref, True, store)
+    fill_margins(buffer, gated_ref[0])
+
+    @pl.when(pl.program_id(1) == 0)
+    def _():
+        taps_ref[...] = jnp.zeros((KERNEL + 1, LANES), jnp.float32)
+
+    for phase in range(8):
+        totals = [jnp.zeros((8, LANES), jnp.float32)] * 4
+        for begin in range(0, ROWS, LANES):
+            span = buffer[begin + phase : begin + phase + LANES + 24, :]
+            grad = grad_ref[0, begin : begin + LANES, :]
+            for block in range(4):
+                if 8 * block + phase == 0:
+                    continue
+                both = grad * span[8 * block : 8 * block + LANES]
+                totals[block] += jnp.sum(both.reshape(LANES // 8, 8, LANES), axis=0)
+        for block in range(4):
+            tap = 8 * block + phase - 1
+            if tap >= 0:
+                taps_ref[tap : tap + 1, :] += jnp.sum(totals[block], axis=0, keepdims=True)
+
+
+def lane_block(rows):
+    return pl.BlockSpec((1, rows, LANES), lambda lane, clip: (clip, 0, lane))
+
+
+def line_block(rows):
+    return pl.BlockSpec((rows, LANES), lambda lane, clip: (0, lane))
+
+
+def depthwise(gated, lines):
+    clip_count = gated.shape[0]
+    return pl.pallas_call(
+        depthwise_kernel,
+        grid=(D // LANES, clip_count),
+        in_specs=[lane_block(ROWS), line_block(lines.shape[0])],
+        out_specs=[lane_block(ROWS), lane_block(8)],
+        out_shape=[
+            jax.ShapeDtypeStruct((clip_count, ROWS, D), jnp.float32),
+            jax.ShapeDtypeStruct((clip_count, 8, D), jnp.float32),
+        ],
+        scratch_shapes=[pltpu.VMEM((ROWS + 2 * MARGIN, LANES), jnp.float32)],
+    )(gated, lines)
+
+
+def depthwise_back(grad_out, gated, lines):
+    clip_count = gated.shape[0]
+    grad_gated, taps = pl.pallas_call(
+        depthwise_back_kernel,
+        grid=(D // LANES, clip_count),
+        in_specs=[lane_block(ROWS), lane_block(ROWS), line_block(lines.shape[0])],
+        out_specs=[lane_block(ROWS), line_block(KERNEL + 1)],
+        out_shape=[
+            jax.ShapeDtypeStruct((clip_count, ROWS, D), jnp.float32),
+            jax.ShapeDtypeStruct((KERNEL + 1, D), jnp.float32),
+        ],
+        scratch_shapes=[pltpu.VMEM((ROWS + 2 * MARGIN, LANES), jnp.float32)],
+    )(grad_out, gated, lines)
+    return grad_gated, taps[:KERNEL]
+
+
+def swap(piece, axis, bit):
+    size = lax.axis_size(axis)
+    return lax.ppermute(piece, axis, [(place, place ^ bit) for place in range(size)])
+
+
+def bits(axis):
+    bit = 1
+    while bit < lax.axis_size(axis):
+        yield bit
+        bit *= 2
+
+
+def is_high(axis, bit):
+    return (lax.axis_index(axis) // bit) % 2 == 1
+
+
+def sum_everywhere(piece):
+    for axis in ("rep", "shard"):
+        for bit in bits(axis):
+            piece = piece + swap(piece, axis, bit)
+    return piece
+
+
+def moments_everywhere(mean, square, count):
+    for axis in ("rep", "shard"):
+        for bit in bits(axis):
+            other = swap(jnp.concatenate([mean, square], axis=0), axis, bit)
+            apart = mean - other[:1]
+            square = square + other[1:] + apart * apart * (0.5 * count)
+            mean = 0.5 * (mean + other[:1])
+            count = 2.0 * count
+    return mean, square, count
+
+
+def keep_half(low, high, axis, bit):
+    upper = is_high(axis, bit)
+    sent = jnp.where(upper, low, high).astype(jnp.bfloat16)
+    kept = jnp.where(upper, high, low)
+    return kept + swap(sent, axis, bit).astype(jnp.float32)
+
+
+def reduce_piece(piece):
+    shard_count = lax.axis_size("shard")
+    rows = piece.shape[0] // shard_count
+    for bit in bits("rep"):
+        half = piece.shape[1] // 2
+        piece = keep_half(piece[:, :half], piece[:, half:], "rep", bit)
+    cols = piece.shape[1]
+    for bit in bits("shard"):
+        left = piece.shape[0] // rows
+        view = piece.reshape(left // 2, 2, rows, cols)
+        piece = keep_half(view[:, 0], view[:, 1], "shard", bit).reshape(left // 2 * rows, cols)
+    piece = piece.astype(jnp.bfloat16)
+    for bit in reversed(list(bits("rep"))):
+        other = swap(piece, "rep", bit)
+        upper = is_high("rep", bit)
+        piece = jnp.concatenate(
+            [jnp.where(upper, other, piece), jnp.where(upper, piece, other)], axis=1
         )
-        kernel_rows.append(
-            jnp.sum(grad_out * padded_gated[:, tap_index : tap_index + ROWS, :], axis=(0, 1))
+    return piece.astype(jnp.float32)
+
+
+def gather_piece(piece):
+    rows, cols = piece.shape
+    shape = (1, rows, cols)
+    piece = piece.reshape(shape)
+    for bit in reversed(list(bits("shard"))):
+        other = swap(piece, "shard", bit)
+        upper = is_high("shard", bit)
+        piece = jnp.stack(
+            [jnp.where(upper, other, piece), jnp.where(upper, piece, other)], axis=1
+        ).reshape(-1, rows, cols)
+    return piece.reshape(-1, cols)
+
+
+def gather_quarter(piece):
+    cols = piece.shape[1]
+    for bit in bits("rep"):
+        half = piece.shape[1] // 2
+        piece = jnp.where(is_high("rep", bit), piece[:, half:], piece[:, :half])
+    piece = gather_piece(piece)
+    for bit in reversed(list(bits("rep"))):
+        other = swap(piece, "rep", bit)
+        upper = is_high("rep", bit)
+        piece = jnp.concatenate(
+            [jnp.where(upper, other, piece), jnp.where(upper, piece, other)], axis=1
         )
-    return (grad_gated, jnp.stack(kernel_rows))
+    return piece
 
 
 def ffn_forward(residual, w_in, bias_in, w_out, vector_full, first_row):
@@ -434,25 +619,22 @@
     )
     normed = normed.astype(jnp.bfloat16)
     glu_pre = product(normed, w_glu) + jnp.concatenate(
-        [vector_full[glu_value], vector_full[glu_gate]]
+        [vector_full[glu_value], vector_full[glu_gate]], axis=1
     )
     value_half = glu_pre[:, :D]
     gate_logistic = jax.nn.sigmoid(glu_pre[:, D:])
     valid = valid_rows(clip_count)
     gated = jnp.where(valid, (value_half * gate_logistic).reshape(clip_count, ROWS, D), 0.0)
-    kernel = vector_full[kernel_start : kernel_start + KERNEL]
-    depth_out = depthwise(gated, kernel)
-    local_count = float(clip_count * CLIP_LEN)
-    device_count = lax.axis_size("rep") * lax.axis_size("shard")
-    token_count = device_count * local_count
-    local_mean = jnp.sum(jnp.where(valid, depth_out, 0.0), axis=(0, 1)) / local_count
+    depth_out, stats = depthwise(gated, vector_full.whole)
+    clip_mean, clip_square = stats[:, 0], stats[:, 1]
+    local_mean = jnp.mean(clip_mean, axis=0, keepdims=True)
     local_square = jnp.sum(
-        jnp.where(valid, (depth_out - local_mean) ** 2, 0.0), axis=(0, 1)
-    )
-    both = lax.all_gather(jnp.stack([local_mean, local_square]), ("rep", "shard"))
-    mean_depth = jnp.mean(both[:, 0], axis=0)
-    between = jnp.sum((both[:, 0] - mean_depth) ** 2, axis=0) * local_count
-    var_depth = (jnp.sum(both[:, 1], axis=0) + between) / token_count
+        clip_square + CLIP_LEN * (clip_mean - local_mean) ** 2, axis=0, keepdims=True
+    )
+    mean_depth, square_depth, token_count = moments_everywhere(
+        local_mean, local_square, float(clip_count * CLIP_LEN)
+    )
+    var_depth = square_depth / token_count
     centered = depth_out - mean_depth
     inverse_batch = lax.rsqrt(var_depth + norm_eps)
     unit_batch = centered * inverse_batch
@@ -499,9 +681,8 @@
     grad_norm = grad_active * swish_slope(normed_batch)
     local_shift = jnp.sum(grad_norm, axis=(0, 1))
     local_gain = jnp.sum(grad_norm * unit_batch, axis=(0, 1))
-    total_shift, overall_multiplier = lax.psum(
-        jnp.stack([local_shift, local_gain]), ("rep", "shard")
-    )
+    totals = sum_everywhere(jnp.stack([local_shift, local_gain]))
+    total_shift, overall_multiplier = totals[:1], totals[1:]
     valid = valid_rows(clip_count)
     grad_depth = (
         vector_full[batch_gain]
@@ -509,9 +690,8 @@
         * (grad_norm - total_shift / token_count - unit_batch * (overall_multiplier / token_count))
     )
     grad_depth = jnp.where(valid, grad_depth, 0.0)
-    kernel = vector_full[kernel_start : kernel_start + KERNEL]
-    grad_gated, grad_kernel = depthwise_back(grad_depth, gated, kernel)
-    grad_gated = jnp.where(valid, grad_gated, 0.0).reshape(row_count, D)
+    grad_gated, grad_kernel = depthwise_back(grad_depth, gated, vector_full.whole)
+    grad_gated = grad_gated.reshape(row_count, D)
     grad_value = grad_gated * gate_logistic
     grad_gate = grad_gated * value_half * gate_logistic * (1.0 - gate_logistic)
     glu_low = jnp.concatenate([grad_value, grad_gate], axis=1).astype(jnp.bfloat16)
@@ -578,15 +758,18 @@
     def gather(piece):
         return lax.all_gather(piece, "shard", axis=0, tiled=True)
 
-    small = lax.all_gather(
-        jnp.concatenate([vectors, hidden_bias.reshape(hidden_lines, vector_cols)], axis=0), "shard"
-    ).astype(jnp.float32)
-    vector_full = small[:, :row_total].transpose(1, 0, 2).reshape(row_total, D)
-    hidden_full = (
+    w_front = gather_quarter(row_weights[:, :FF])
+    down_front = gather_quarter(down_weights[0])
+    small = gather_piece(
+        jnp.concatenate([vectors, hidden_bias.reshape(hidden_lines, vector_cols)], axis=0)
+    )
+    small = small.reshape(shard_count, -1, vector_cols).astype(jnp.float32)
+    vector_full = Lines(
+        lax.optimization_barrier(small[:, :row_total].transpose(1, 0, 2).reshape(row_total, D))
+    )
+    hidden_full = Lines(
         small[:, row_total:].reshape(shard_count, 2, hidden_cols).transpose(1, 0, 2).reshape(2, FF)
     )
-    w_front = gather(row_weights[:, :FF])
-    down_front = gather(down_weights[0])
     w_rest = gather(row_weights[:, offset_cols:])
     w_back = gather(row_weights[:, FF:offset_cols])
     down_back = gather(down_weights[1])
@@ -633,19 +816,12 @@
         + [back_grads[3], back_grads[4], back_grads[5], final_gain_grad, final_shift_grad]
     )
     vector_grad = jnp.concatenate([jnp.stack(vector_rows), conv_grads[9]], axis=0)
-
-    def reduce(piece):
-        piece = lax.psum_scatter(
-            piece.astype(jnp.bfloat16), "shard", scatter_dimension=0, tiled=True
-        )
-        return lax.psum(piece, "rep").astype(jnp.float32)
-
-    back_sum = reduce(back_grads[0])
-    down_back_sum = reduce(back_grads[2])
-    conv_sum = reduce(jnp.concatenate([conv_grads[0], attend_grad, conv_grads[1]], axis=1))
-    attend_sum = reduce(jnp.concatenate([triple_grad, place_grad], axis=1))
-    down_front_sum = reduce(front_grads[2])
-    front_sum = reduce(front_grads[0])
+    back_sum = reduce_piece(back_grads[0])
+    down_back_sum = reduce_piece(back_grads[2])
+    conv_sum = reduce_piece(jnp.concatenate([conv_grads[0], attend_grad, conv_grads[1]], axis=1))
+    attend_sum = reduce_piece(jnp.concatenate([triple_grad, place_grad], axis=1))
+    down_front_sum = reduce_piece(front_grads[2])
+    front_sum = reduce_piece(front_grads[0])
     small_grad = jnp.concatenate(
         [
             vector_grad.reshape(row_total, shard_count, vector_cols).transpose(1, 0, 2),
@@ -655,7 +831,9 @@
         ],
         axis=1,
     )
-    small_sum = lax.psum(small_grad, ("rep", "shard"))[lax.axis_index("shard")]
+    small_sum = lax.dynamic_index_in_dim(
+        sum_everywhere(small_grad), lax.axis_index("shard"), 0, keepdims=False
+    )
     owned_grads = (
         jnp.concatenate([front_sum, back_sum, attend_sum, conv_sum], axis=1),
         jnp.stack([down_front_sum, down_back_sum]),

time: 1130 us -> 670 us (0.59)
  waiting for transfers between devices: 453 us -> 152 us
  blocking collectives: 137 us -> 0 us
  local copies, waits for them, and re-layouts: 135 us -> 72.9 us
  starting transfers between devices: 0.71 us -> 61.7 us
  Pallas kernels: 105 us -> 132 us
  other arithmetic: 128 us -> 102 us
  matrix products: 145 us -> 129 us
    reduce_scatter x6 -> x0, waiting for transfers between devices: 277 us -> none  [reduce(): lax.psum_scatter(piece.astype(jnp.bfloat16), 'shard', scatter_dimension=0...]
    psum x2 -> x0, waiting for transfers between devices: 161 us -> none  [the longest x1 119 us: shards(): small_sum = lax.psum(small_grad, ('rep', 'shard'))[lax.axis_index('shard')]]
    ppermute x0 -> x70, waiting for transfers between devices: none -> 138 us  [swap(): lax.ppermute(piece, axis, [(place, place ^ bit) for place in range(size)])]
    all_gather x2 -> x0, blocking collectives: 100 us -> none  [the longest x1 66.8 us: conv_forward(): lax.all_gather(jnp.stack([local_mean, local_square]), ('rep', 'shard'))]
    ppermute x0 -> x70, starting transfers between devices: none -> 61.6 us  [swap(): lax.ppermute(piece, axis, [(place, place ^ bit) for place in range(size)])]
    reduce_sum x6 -> x2, other arithmetic: 51.1 us -> 0.04 us  [the longest x1 0.02 us: conv_forward(): jnp.sum(clip_square + CLIP_LEN * (clip_mean - local_mean) ** 2, axis=0, k...]
    mul x37 -> x0, local copies, waits for them, and re-layouts: 47.9 us -> none  [the longest x31 41.2 us: depthwise(): kernel[tap_index] * padded[:, tap_index:tap_index + ROWS, :]]
    psum x1 -> x0, blocking collectives: 37.3 us -> none  [conv_backward(): lax.psum(jnp.stack([local_shift, local_gain]), ('rep', 'shard'))]
  transfers between devices with their start and end apart: 13 -> 73, of which waited for: 7 -> 35; matrix products, arithmetic and copies ran while one was open for 26% -> 37% of each run, Pallas kernels for 9% -> 20%
where the time goes in v1:
time: 670 us; the launch traced here: 667 us
  waiting for transfers between devices  152 us (23%)
  Pallas kernels  132 us (20%)
  matrix products  129 us (19%)
  other arithmetic  102 us (15%)
  local copies, waits for them, and re-layouts  72.9 us (11%)
  starting transfers between devices  61.7 us (9%)
  between operations  17.9 us (3%)
    ppermute x70, waiting for transfers between devices, swap(): lax.ppermute(piece, axis, [(place, place ^ bit) for place in range(size)])  138 us
    pallas_call x1, Pallas kernels, attend_back_call(): pl.pallas_call(attend_back_kernel, grid=(PAIRS, clip_count), in_specs=[cl...  69.1 us
    ppermute x70, starting transfers between devices, swap(): lax.ppermute(piece, axis, [(place, place ^ bit) for place in range(size)])  61.6 us
    dot_general x8, matrix products, product_right(): lax.dot_general(left, right, (((1,), (1,)), ((), ())), preferred_element_...  47.1 us
    dot_general x8, matrix products, product(): return jnp.dot(left, right, preferred_element_type=jnp.float32)  45.3 us
    dot_general x8, matrix products, left_factor(): lax.dot_general(left, right, (((0,), (0,)), ((), ())), preferred_element_...  36.8 us
    pallas_call x1, Pallas kernels, attend_call(): pl.pallas_call(attend_kernel, grid=(PAIRS, clip_count), in_specs=[clip_bl...  36 us
    unnamed x306, local copies, waits for them, and re-layouts  26.5 us
  transfers between devices with their start and end apart: 73, of which 35 were waited for; matrix products, arithmetic and copies ran while one was open for 37% of the time, Pallas kernels for 20%

profile of v1, /device:TPU:0, one launch (start us, length us, event | category | flops | bytes accessed | tf_op | source)
XLA Modules:
  0.0 666.7 jit_solution(13342434194686335191)
XLA Ops:
  57.2 12.1 %collective-permute-done.4 = bf16[2,64,512]{2,1,0:T(8,128)(2,1)S(1)} collective-permute-done((bf16[2,64,512]{2,1,0:T(8,128)(2,1)S(1)}, bf16[2,64,512]{2,1,0:T(8,128)(2,1)S(1)}, u32[]{:S(2)}, u32[]{:S(2)}) %collective-permute-start.4) | collective-permute-done | bytes 131104 | tf_op jit(solution)/shard_map/ppermute | solution.py:417
  69.4 6.6 collective-permute-done.9
  86.6 8.0 %collective-permute-done.6 = bf16[512,512]{1,0:T(8,128)(2,1)} collective-permute-done((bf16[512,512]{1,0:T(8,128)(2,1)}, bf16[512,512]{1,0:T(8,128)(2,1)}, u32[]{:S(2)}, u32[]{:S(2)}) %collective-permute-start.6) | collective-permute-done | bytes 524320 | tf_op jit(solution)/shard_map/ppermute | solution.py:417
  96.1 7.4 %collective-permute-done.11 = bf16[2048,128]{1,0:T(8,128)(2,1)S(1)} collective-permute-done((bf16[2048,128]{1,0:T(8,128)(2,1)S(1)}, bf16[2048,128]{1,0:T(8,128)(2,1)S(1)}, u32[]{:S(2)}, u32[]{:S(2)}) %collective-permute-start.11) | collective-permute-done | bytes 524320 | tf_op jit(solution)/shard_map/ppermute | solution.py:417
  105.1 8.5 %multiply_convert_fusion.1 = (bf16[1536,2048]{1,0:T(8,128)(2,1)S(1)}, f32[1536,2048]{1,0:T(8,128)}) fusion(f32[2048]{0:T(1024)S(1)} %bitcast.694, bf16[1536,512]{1,0:T(8,128)(2,1)S(1)} %copy-done.47, bf16[512,1024]{1,0:T(8,128)(2,1)S(1)} %get-tuple-element.102, bf16[512,1024]{1,0:T(8,128)(2,1)S(1)} %get-tuple-element.101), kind=kOutput, calls=%fused_computation.4 | convolution fusion | flops 3244294144 | bytes 22552576 | tf_op jit(solution)/shard_map/dot_general | solution.py:60
  133.1 36.0 %shard_map.286 = (bf16[2,768,512]{2,1,0:T(8,128)(2,1)}, f32[2,4,2,768]{3,2,1,0:T(2,128)}) custom-call(bf16[2,768,512]{2,1,0:T(8,128)(2,1)} %bitcast.592, bf16[2,768,512]{2,1,0:T(8,128)(2,1)} %bitcast.590, bf16[2,768,512]{2,1,0:T(8,128)(2,1)} %bitcast.596, bf16[2,768,512]{2,1,0:T(8,128)(2,1)} %bitcast.594, bf16[512,512]{1,0:T(8,128)(2,1)} %pad_maximum_fusion.19.place_ref, ...), custom_call_target="tpu_custom_call" | custom-call | tf_op jit(solution)/shard_map/pallas_call | solution.py:251
  180.7 9.8 %shard_map.287 = (f32[2,768,512]{2,1,0:T(8,128)}, f32[2,8,512]{2,1,0:T(8,128)}) custom-call(f32[2,768,512]{2,1,0:T(8,128)} %broadcast_select_fusion.gated_ref, f32[53,512]{1,0:T(8,128)} %copy-done.52), custom_call_target="tpu_custom_call" | custom-call | tf_op jit(solution)/shard_map/pallas_call | solution.py:386
  225.7 11.3 %multiply_convert_fusion = (bf16[1536,2048]{1,0:T(8,128)(2,1)}, f32[1536,2048]{1,0:T(8,128)}) fusion(f32[2048]{0:T(1024)S(1)} %bitcast.697, bf16[512,2048]{1,0:T(8,128)(2,1)} %all-gather.7.cloned.1.call-done, f32[1536,512]{1,0:T(8,128)} %copy-done.12, f32[512]{0:T(512)S(1)} %bitcast.708, f32[512]{0:T(512)S(1)} %bitcast.686, f32[1536]{0:T(1024)S(1)} %add_rsqrt_fusion.2, ...), kind=kOutput, calls=%fused_computation.2 | convolution fusion | flops 3244032000 | bytes 24141824 | tf_op jit(solution)/shard_map/dot_general | solution.py:60
  237.0 13.9 %all-gather.9.cloned.1.call-done = bf16[1,2048,512]{2,1,0:T(8,128)(2,1)} async-done(((bf16[1,256,512]{2,1,0:T(8,128)(2,1)}), bf16[1,2048,512]{2,1,0:T(8,128)(2,1)}) %all-gather.9.cloned.1.call-update) | async-done | bytes 2097168 | tf_op jit(solution)/shard_map/all_gather | solution.py:759
  250.9 8.1 %fusion.130 = (f32[1536]{0:T(1024)S(1)}, f32[1536,512]{1,0:T(8,128)S(1)}) fusion(f32[1536,512]{1,0:T(8,128)} %copy-done.12, f32[512]{0:T(512)S(1)} %bitcast.710, bf16[1536,2048]{1,0:T(8,128)(2,1)} %get-tuple-element.194, bf16[1,2048,512]{2,1,0:T(8,128)(2,1)} %all-gather.9.cloned.1.call-done), kind=kOutput, calls=%fused_computation.442 | convolution fusion | flops 3224369664 | bytes 14688256 | tf_op jit(solution)/shard_map/dot_general | solution.py:60
  273.7 9.1 %fusion.131 = (f32[2048]{0:T(1024)S(1)}, bf16[1536,2048]{1,0:T(8,128)(2,1)S(1)}) fusion(f32[1536,2048]{1,0:T(8,128)} %get-tuple-element.195, f32[2048]{0:T(1024)S(1)} %bitcast.698, bf16[1,2048,512]{2,1,0:T(8,128)(2,1)S(1)} %copy-done.141, f32[1536,512]{1,0:T(8,128)S(1)} %get-tuple-element.83), kind=kOutput, calls=%fused_computation.443 | convolution fusion | flops 3257399296 | bytes 24133632 | tf_op jit(solution)/shard_map/dot_general | solution.py:70
  295.7 5.6 fusion.18
  330.5 16.6 %shard_map.288 = (f32[2,768,512]{2,1,0:T(8,128)}, f32[32,512]{1,0:T(8,128)}) custom-call(f32[2,768,512]{2,1,0:T(8,128)} %multiply_select_fusion.grad_ref, f32[2,768,512]{2,1,0:T(8,128)} %broadcast_select_fusion.gated_ref, f32[53,512]{1,0:T(8,128)} %copy-done.52), custom_call_target="tpu_custom_call" | custom-call | tf_op jit(solution)/shard_map/pallas_call | solution.py:401
  363.7 69.1 %shard_map.289 = (bf16[2,768,512]{2,1,0:T(8,128)(2,1)}, bf16[2,768,512]{2,1,0:T(8,128)(2,1)}, bf16[2,768,512]{2,1,0:T(8,128)(2,1)}, f32[2,4,8,128]{3,2,1,0:T(8,128)}, f32[512,512]{1,0:T(8,128)}) custom-call(bf16[2,768,512]{2,1,0:T(8,128)(2,1)} %bitcast.593, bf16[2,768,512]{2,1,0:T(8,128)(2,1)} %bitcast.591, bf16[2,768,512]{2,1,0:T(8,128)(2,1)} %bitcast.597, ...), custom_call_target="tpu_custom_call" | custom-call | tf_op jit(solution)/shard_map/pallas_call | solution.py:275
  432.9 7.9 %fusion.27 = f32[512,1536]{1,0:T(8,128)} fusion(bf16[1536,512]{1,0:T(8,128)(2,1)} %bitcast.715, bf16[1536,512]{1,0:T(8,128)(2,1)} %bitcast.713, bf16[1536,512]{1,0:T(8,128)(2,1)} %bitcast.711, f32[1536,512]{1,0:T(8,128)} %copy-done.9, f32[512]{0:T(512)S(1)} %bitcast.706, f32[512]{0:T(512)S(1)} %bitcast.678, f32[1536]{0:T(1024)S(1)} %copy-done.93, ...), kind=kOutput, calls=%fused_computation.116 | convolution fusion | flops 2434007040 | bytes 11026432 | tf_op jit(solution)/shard_map/dot_general | solution.py:64
  453.4 10.0 %fusion.132 = (f32[2048]{0:T(1024)S(1)}, bf16[1536,2048]{1,0:T(8,128)(2,1)S(1)}) fusion(f32[1536,2048]{1,0:T(8,128)} %get-tuple-element.187, f32[2048]{0:T(1024)S(1)} %bitcast.695, bf16[2048,256]{1,0:T(8,128)(2,1)S(1)} %copy-done.64, bf16[2048,256]{1,0:T(8,128)(2,1)S(1)} %copy-done.62, f32[1536,512]{1,0:T(8,128)S(1)} %get-tuple-element.89), kind=kOutput, calls=%fused_computation.444 | convolution fusion | flops 3261593600 | bytes 24133632 | tf_op jit(solution)/shard_map/dot_general | solution.py:70
  463.5 6.8 %multiply_reduce_fusion.3 = (f32[512]{0:T(512)S(1)}, f32[1536]{0:T(1024)}, f32[1536]{0:T(1024)}, f32[512]{0:T(512)S(1)}, f32[1536,512]{1,0:T(8,128)}) fusion(f32[2,768,512]{2,1,0:T(8,128)S(1)} %copy-done.7, f32[1536]{0:T(1024)S(1)} %copy-done.72, f32[1536]{0:T(1024)S(1)} %copy-done.74, f32[512]{0:T(512)S(1)} %bitcast.669, ...), kind=kOutput, calls=%fused_computation.40 | convolution fusion | flops 3232493568 | bytes 14710784 | tf_op jit(solution)/shard_map/dot_general | solution.py:70
  500.9 6.6 collective-permute-done.66
  508.2 6.8 %collective-permute-done.67 = f32[8,61,64]{2,1,0:T(8,128)S(1)} collective-permute-done((f32[8,61,64]{2,1,0:T(8,128)S(1)}, f32[8,61,64]{2,1,0:T(8,128)S(1)}, u32[]{:S(2)}, u32[]{:S(2)}) %collective-permute-start.67) | collective-permute-done | bytes 124960 | tf_op jit(solution)/shard_map/ppermute | solution.py:417
  556.1 10.5 %collective-permute-done.31 = bf16[512,512]{1,0:T(8,128)(2,1)S(1)} collective-permute-done((bf16[512,512]{1,0:T(8,128)(2,1)S(1)}, bf16[512,512]{1,0:T(8,128)(2,1)S(1)}, u32[]{:S(2)}, u32[]{:S(2)}) %collective-permute-start.31) | collective-permute-done | bytes 524320 | tf_op jit(solution)/shard_map/ppermute | solution.py:417
  567.5 10.4 %collective-permute-done.52 = bf16[2048,128]{1,0:T(8,128)(2,1)S(1)} collective-permute-done((bf16[2048,128]{1,0:T(8,128)(2,1)S(1)}, bf16[2048,128]{1,0:T(8,128)(2,1)S(1)}, u32[]{:S(2)}, u32[]{:S(2)}) %collective-permute-start.52) | collective-permute-done | bytes 524320 | tf_op jit(solution)/shard_map/ppermute | solution.py:417
  578.6 10.5 %collective-permute-done.45 = bf16[512,512]{1,0:T(8,128)(2,1)S(1)} collective-permute-done((bf16[512,512]{1,0:T(8,128)(2,1)S(1)}, bf16[512,512]{1,0:T(8,128)(2,1)S(1)}, u32[]{:S(2)}, u32[]{:S(2)}) %collective-permute-start.45) | collective-permute-done | bytes 524320 | tf_op jit(solution)/shard_map/ppermute | solution.py:417
  589.9 10.4 %collective-permute-done.38 = bf16[512,512]{1,0:T(8,128)(2,1)S(1)} collective-permute-done((bf16[512,512]{1,0:T(8,128)(2,1)S(1)}, bf16[512,512]{1,0:T(8,128)(2,1)S(1)}, u32[]{:S(2)}, u32[]{:S(2)}) %collective-permute-start.38) | collective-permute-done | bytes 524320 | tf_op jit(solution)/shard_map/ppermute | solution.py:417
  601.4 9.0 %collective-permute-done.24 = bf16[512,512]{1,0:T(8,128)(2,1)S(1)} collective-permute-done((bf16[512,512]{1,0:T(8,128)(2,1)S(1)}, bf16[512,512]{1,0:T(8,128)(2,1)S(1)}, u32[]{:S(2)}, u32[]{:S(2)}) %collective-permute-start.24) | collective-permute-done | bytes 524320 | tf_op jit(solution)/shard_map/ppermute | solution.py:417
  (718 shorter events, 337.8 us)
Async XLA Ops:
  7.2 113.3 %all-gather.5.cloned.1.call-start = ((), (), s32[]{:S(2)}) async-start(), calls=%async_computation | async-start | bytes 4718592 | tf_op jit(solution)/shard_map/all_gather | solution.py:759
  9.3 216.3 %all-gather.7.cloned.1.call-start = ((), (), s32[]{:S(2)}) async-start(), calls=%async_computation.1 | async-start | bytes 2359296 | tf_op jit(solution)/shard_map/all_gather | solution.py:759
  12.5 41.9 %collective-permute-start.8 = (bf16[1,256,128]{2,1,0:T(8,128)(2,1)}, bf16[1,256,128]{2,1,0:T(8,128)(2,1)}, u32[]{:S(2)}, u32[]{:S(2)}) collective-permute-start(bf16[1,256,128]{2,1,0:T(8,128)(2,1)} %fusion.88), channel_id=1, source_target_pairs={{0,4},{1,5},{2,6},{3,7},{4,0},{5,1},{6,2},{7,3},{8,12},{9,13},{10,... | collective-permute-start | bytes 196616 | tf_op jit(solution)/shard_map/ppermute | solution.py:417
  17.9 35.4 %collective-permute-start.3 = (bf16[1,64,512]{2,1,0:T(8,128)(2,1)}, bf16[1,64,512]{2,1,0:T(8,128)(2,1)}, u32[]{:S(2)}, u32[]{:S(2)}) collective-permute-start(bf16[1,64,512]{2,1,0:T(8,128)(2,1)} %fusion.89), channel_id=1, source_target_pairs={{0,4},{1,5},{2,6},{3,7},{4,0},{5,1},{6,2},{7,3},{8,12},{9,13},{10,... | collective-permute-start | bytes 196616 | tf_op jit(solution)/shard_map/ppermute | solution.py:417
  22.3 228.6 %all-gather.9.cloned.1.call-start = ((), (), s32[]{:S(2)}) async-start(), calls=%async_computation.2 | async-start | bytes 2359296 | tf_op jit(solution)/shard_map/all_gather | solution.py:759
  54.2 15.1 %collective-permute-start.4 = (bf16[2,64,512]{2,1,0:T(8,128)(2,1)S(1)}, bf16[2,64,512]{2,1,0:T(8,128)(2,1)S(1)}, u32[]{:S(2)}, u32[]{:S(2)}) collective-permute-start(bf16[2,64,512]{2,1,0:T(8,128)(2,1)S(1)} %maximum_bitcast_fusion), channel_id=1, source_target_pairs={{0,2},{1,3},{2,0},{3,1},{4,6},{5,7},{6,4},{7,5},{8,10},{9,11},{10,... | collective-permute-start | bytes 393224 | tf_op jit(solution)/shard_map/ppermute | solution.py:417
  55.2 20.7 %collective-permute-start.9 = (bf16[2,256,128]{2,1,0:T(8,128)(2,1)S(1)}, bf16[2,256,128]{2,1,0:T(8,128)(2,1)S(1)}, u32[]{:S(2)}, u32[]{:S(2)}) collective-permute-start(bf16[2,256,128]{2,1,0:T(8,128)(2,1)S(1)} %maximum_bitcast_fusion.1), channel_id=1, source_target_pairs={{0,2},{1,3},{2,0},{3,1},{4,6},{5,7},{6,4},{7,5},{8,10},{9,11},{10,... | collective-permute-start | bytes 393224 | tf_op jit(solution)/shard_map/ppermute | solution.py:417
  79.5 15.1 %collective-permute-start.6 = (bf16[512,512]{1,0:T(8,128)(2,1)}, bf16[512,512]{1,0:T(8,128)(2,1)}, u32[]{:S(2)}, u32[]{:S(2)}) collective-permute-start(bf16[512,512]{1,0:T(8,128)(2,1)} %bitcast.25), channel_id=1, source_target_pairs={{0,16},{8,24},{16,0},{24,8},{1,17},{9,25},{17,1},{25,9},{2,18},{10... | collective-permute-start | bytes 1572872 | tf_op jit(solution)/shard_map/ppermute | solution.py:417
  85.1 18.5 %collective-permute-start.11 = (bf16[2048,128]{1,0:T(8,128)(2,1)S(1)}, bf16[2048,128]{1,0:T(8,128)(2,1)S(1)}, u32[]{:S(2)}, u32[]{:S(2)}) collective-permute-start(bf16[2048,128]{1,0:T(8,128)(2,1)S(1)} %bitcast.633), channel_id=1, source_target_pairs={{0,16},{8,24},{16,0},{24,8},{1,17},{9,25},{17,1},{25,9},{2,18},{10... | collective-permute-start | bytes 1572872 | tf_op jit(solution)/shard_map/ppermute | solution.py:417
  319.1 217.5 %collective-permute-start.58 = (bf16[2048,256]{1,0:T(8,128)(2,1)}, bf16[2048,256]{1,0:T(8,128)(2,1)}, u32[]{:S(2)}, u32[]{:S(2)}) collective-permute-start(bf16[2048,256]{1,0:T(8,128)(2,1)} %select_convert_fusion), channel_id=1, source_target_pairs={{0,8},{8,0},{16,24},{24,16},{1,9},{9,1},{17,25},{25,17},{2,10},{10... | collective-permute-start | bytes 3145736 | tf_op jit(solution)/shard_map/ppermute | solution.py:417
  323.5 217.0 %collective-permute-start.30 = (bf16[512,1024]{1,0:T(8,128)(2,1)}, bf16[512,1024]{1,0:T(8,128)(2,1)}, u32[]{:S(2)}, u32[]{:S(2)}) collective-permute-start(bf16[512,1024]{1,0:T(8,128)(2,1)} %select_convert_fusion.4), channel_id=1, source_target_pairs={{0,8},{8,0},{16,24},{24,16},{1,9},{9,1},{17,25},{25,17},{2,10},{10... | collective-permute-start | bytes 3145736 | tf_op jit(solution)/shard_map/ppermute | solution.py:417
  490.3 53.1 %collective-permute-start.51 = (bf16[2048,256]{1,0:T(8,128)(2,1)}, bf16[2048,256]{1,0:T(8,128)(2,1)}, u32[]{:S(2)}, u32[]{:S(2)}) collective-permute-start(bf16[2048,256]{1,0:T(8,128)(2,1)} %select_convert_fusion.1), channel_id=1, source_target_pairs={{0,8},{8,0},{16,24},{24,16},{1,9},{9,1},{17,25},{25,17},{2,10},{10... | collective-permute-start | bytes 3145736 | tf_op jit(solution)/shard_map/ppermute | solution.py:417
  495.9 50.5 %collective-permute-start.44 = (bf16[512,1024]{1,0:T(8,128)(2,1)}, bf16[512,1024]{1,0:T(8,128)(2,1)}, u32[]{:S(2)}, u32[]{:S(2)}) collective-permute-start(bf16[512,1024]{1,0:T(8,128)(2,1)} %get-tuple-element.202), channel_id=1, source_target_pairs={{0,8},{8,0},{16,24},{24,16},{1,9},{9,1},{17,25},{25,17},{2,10},{10... | collective-permute-start | bytes 3145736 | tf_op jit(solution)/shard_map/ppermute | solution.py:417
  536.7 16.1 %collective-permute-start.23 = (bf16[512,1024]{1,0:T(8,128)(2,1)}, bf16[512,1024]{1,0:T(8,128)(2,1)S(1)}, u32[]{:S(2)}, u32[]{:S(2)}) collective-permute-start(bf16[512,1024]{1,0:T(8,128)(2,1)} %select_convert_fusion.5), channel_id=1, source_target_pairs={{0,8},{8,0},{16,24},{24,16},{1,9},{9,1},{17,25},{25,17},{2,10},{10... | collective-permute-start | bytes 3145736 | tf_op jit(solution)/shard_map/ppermute | solution.py:417
  540.5 14.9 %collective-permute-start.59 = (bf16[2048,128]{1,0:T(8,128)(2,1)S(1)}, bf16[2048,128]{1,0:T(8,128)(2,1)S(1)}, u32[]{:S(2)}, u32[]{:S(2)}) collective-permute-start(bf16[2048,128]{1,0:T(8,128)(2,1)S(1)} %select_convert_fusion.6), channel_id=1, source_target_pairs={{0,16},{8,24},{16,0},{24,8},{1,17},{9,25},{17,1},{25,9},{2,18},{10... | collective-permute-start | bytes 1572872 | tf_op jit(solution)/shard_map/ppermute | solution.py:417
  543.4 23.1 %collective-permute-start.31 = (bf16[512,512]{1,0:T(8,128)(2,1)S(1)}, bf16[512,512]{1,0:T(8,128)(2,1)S(1)}, u32[]{:S(2)}, u32[]{:S(2)}) collective-permute-start(bf16[512,512]{1,0:T(8,128)(2,1)S(1)} %select_convert_fusion.10), channel_id=1, source_target_pairs={{0,16},{8,24},{16,0},{24,8},{1,17},{9,25},{17,1},{25,9},{2,18},{10... | collective-permute-start | bytes 1572872 | tf_op jit(solution)/shard_map/ppermute | solution.py:417
  546.4 31.5 %collective-permute-start.52 = (bf16[2048,128]{1,0:T(8,128)(2,1)S(1)}, bf16[2048,128]{1,0:T(8,128)(2,1)S(1)}, u32[]{:S(2)}, u32[]{:S(2)}) collective-permute-start(bf16[2048,128]{1,0:T(8,128)(2,1)S(1)} %select_convert_fusion.7), channel_id=1, source_target_pairs={{0,16},{8,24},{16,0},{24,8},{1,17},{9,25},{17,1},{25,9},{2,18},{10... | collective-permute-start | bytes 1572872 | tf_op jit(solution)/shard_map/ppermute | solution.py:417
  549.7 39.4 %collective-permute-start.45 = (bf16[512,512]{1,0:T(8,128)(2,1)S(1)}, bf16[512,512]{1,0:T(8,128)(2,1)S(1)}, u32[]{:S(2)}, u32[]{:S(2)}) collective-permute-start(bf16[512,512]{1,0:T(8,128)(2,1)S(1)} %select_convert_fusion.8), channel_id=1, source_target_pairs={{0,16},{8,24},{16,0},{24,8},{1,17},{9,25},{17,1},{25,9},{2,18},{10... | collective-permute-start | bytes 1572872 | tf_op jit(solution)/shard_map/ppermute | solution.py:417
  552.7 47.6 %collective-permute-start.38 = (bf16[512,512]{1,0:T(8,128)(2,1)S(1)}, bf16[512,512]{1,0:T(8,128)(2,1)S(1)}, u32[]{:S(2)}, u32[]{:S(2)}) collective-permute-start(bf16[512,512]{1,0:T(8,128)(2,1)S(1)} %select_convert_fusion.9), channel_id=1, source_target_pairs={{0,16},{8,24},{16,0},{24,8},{1,17},{9,25},{17,1},{25,9},{2,18},{10... | collective-permute-start | bytes 1572872 | tf_op jit(solution)/shard_map/ppermute | solution.py:417
  555.4 55.1 %collective-permute-start.24 = (bf16[512,512]{1,0:T(8,128)(2,1)S(1)}, bf16[512,512]{1,0:T(8,128)(2,1)S(1)}, u32[]{:S(2)}, u32[]{:S(2)}) collective-permute-start(bf16[512,512]{1,0:T(8,128)(2,1)S(1)} %select_convert_fusion.11), channel_id=1, source_target_pairs={{0,16},{8,24},{16,0},{24,8},{1,17},{9,25},{17,1},{25,9},{2,18},{10... | collective-permute-start | bytes 1572872 | tf_op jit(solution)/shard_map/ppermute | solution.py:417
  566.6 44.8 %collective-permute-start.60 = (bf16[4,256,128]{2,1,0:T(8,128)(2,1)S(1)}, bf16[4,256,128]{2,1,0:T(8,128)(2,1)S(1)}, u32[]{:S(2)}, u32[]{:S(2)}) collective-permute-start(bf16[4,256,128]{2,1,0:T(8,128)(2,1)S(1)} %fusion.57), channel_id=1, source_target_pairs={{0,1},{1,0},{2,3},{3,2},{4,5},{5,4},{6,7},{7,6},{8,9},{9,8},{10,11... | collective-permute-start | bytes 786440 | tf_op jit(solution)/shard_map/ppermute | solution.py:417
  577.8 35.2 %collective-permute-start.32 = (bf16[4,64,512]{2,1,0:T(8,128)(2,1)S(1)}, bf16[4,64,512]{2,1,0:T(8,128)(2,1)S(1)}, u32[]{:S(2)}, u32[]{:S(2)}) collective-permute-start(bf16[4,64,512]{2,1,0:T(8,128)(2,1)S(1)} %fusion.53), channel_id=1, source_target_pairs={{0,1},{1,0},{2,3},{3,2},{4,5},{5,4},{6,7},{7,6},{8,9},{9,8},{10,11... | collective-permute-start | bytes 786440 | tf_op jit(solution)/shard_map/ppermute | solution.py:417
  589.1 24.3 %collective-permute-start.53 = (bf16[4,256,128]{2,1,0:T(8,128)(2,1)S(1)}, bf16[4,256,128]{2,1,0:T(8,128)(2,1)S(1)}, u32[]{:S(2)}, u32[]{:S(2)}) collective-permute-start(bf16[4,256,128]{2,1,0:T(8,128)(2,1)S(1)} %fusion.56), channel_id=1, source_target_pairs={{0,1},{1,0},{2,3},{3,2},{4,5},{5,4},{6,7},{7,6},{8,9},{9,8},{10,11... | collective-permute-start | bytes 786440 | tf_op jit(solution)/shard_map/ppermute | solution.py:417
  600.3 15.2 %collective-permute-start.46 = (bf16[4,64,512]{2,1,0:T(8,128)(2,1)S(1)}, bf16[4,64,512]{2,1,0:T(8,128)(2,1)S(1)}, u32[]{:S(2)}, u32[]{:S(2)}) collective-permute-start(bf16[4,64,512]{2,1,0:T(8,128)(2,1)S(1)} %fusion.55), channel_id=1, source_target_pairs={{0,1},{1,0},{2,3},{3,2},{4,5},{5,4},{6,7},{7,6},{8,9},{9,8},{10,11... | collective-permute-start | bytes 786440 | tf_op jit(solution)/shard_map/ppermute | solution.py:417
  (199 other events, 2122.9 us)
Sparse Core Ops, SparseCore 0:
  10.7 80.8 all-gather.4
  93.8 47.3 all-gather.6
  202.8 47.9 all-gather.8
